TPU v7x, 32 devices: a whole 2x2x4 slice. The times are simulated.
32 devices in a mesh: ctx: 8 (over y, x, core), head: 4 (over z).
Axes of the slice: x: 2, y: 2, z: 4, core: 2. Of those that a mesh axis runs over, the one named last changes fastest.
Arguments:
- queries: bfloat16 [1024, 32, 576], P('ctx', 'head'), may hold values from -512 to 512
- latent: bfloat16 [1024, 576], P(('ctx', 'head')), may hold values from -6 to 6
- out_grad: bfloat16 [1024, 32, 512], P('ctx', 'head'), may hold values from -6 to 6
- segments: int32 [1024], replicated, may hold values from 0 to 3, never falling along the last dimension, each value on 1 to 512 neighbouring positions
Outputs:
- query_grad: bfloat16 [1024, 32, 576], P('ctx', 'head')
- latent_grad: float32 [1024, 576], P(('ctx', 'head'))
All inputs are finite; a program needn't handle non-finite values.
Results may differ from a plain program's by a relative error of at most 0.018.
Values may be sent and summed in bfloat16 or wider, within the bound.
A program may use at most 64 MiB of HBM per device.

v0:
```python
import jax
import jax.numpy as jnp
from jax import lax
from jax.sharding import PartitionSpec as P

WINDOW = 4


score_scale = 192.0 ** (-0.5)


def shifted(value, axis, by):
    peers = lax.axis_size(axis)
    pairs = [(i, i + by) for i in range(peers) if 0 <= i + by < peers]
    return lax.ppermute(value, axis, pairs)


def window_mask(query_index, key_index, query_segments, key_segments):
    causal = (key_index[None, :] >= 0) & (key_index[None, :] <= query_index[:, None])
    return causal & (key_segments[None, :] == query_segments[:, None])


def block_grads(query_rows, key_rows, grad_rows, allowed_mask):
    head_count = query_rows.shape[1]
    value_rank = grad_rows.shape[2]
    query_flat = query_rows.reshape(-1, query_rows.shape[2])
    grad_flat = grad_rows.reshape(-1, value_rank)
    inner_dims = (((1,), (1,)), ((), ()))
    outer_dims = (((0,), (0,)), ((), ()))
    scores = score_scale * lax.dot_general(
        query_flat, key_rows, inner_dims, preferred_element_type=jnp.float32
    )
    expanded = jnp.repeat(allowed_mask, head_count, axis=0)
    scores = jnp.where(expanded, scores, -1e30)
    row_max = jnp.max(scores, axis=1, keepdims=True)
    weights = jnp.where(expanded, jnp.exp(scores - row_max), 0.0)
    soft_probs = weights / jnp.sum(weights, axis=1, keepdims=True)
    probs_half = soft_probs.astype(jnp.bfloat16)
    grad_probs = lax.dot_general(
        grad_flat, key_rows[:, :value_rank], inner_dims, preferred_element_type=jnp.float32
    )
    row_delta = jnp.sum(soft_probs * grad_probs, axis=1, keepdims=True)
    grad_scores = (soft_probs * (grad_probs - row_delta)).astype(jnp.bfloat16)
    grad_query = (
        score_scale * jnp.dot(grad_scores, key_rows, preferred_element_type=jnp.float32)
    ).astype(jnp.bfloat16)
    from_scores = lax.dot_general(
        grad_scores, query_flat, outer_dims, preferred_element_type=jnp.float32
    )
    from_values = lax.dot_general(
        probs_half, grad_flat, outer_dims, preferred_element_type=jnp.float32
    )
    rope_zeros = jnp.zeros((from_values.shape[0], key_rows.shape[1] - value_rank), jnp.float32)
    grad_keys = score_scale * from_scores + jnp.concatenate([from_values, rope_zeros], axis=1)
    return (grad_query.reshape(query_rows.shape), grad_keys)


def shards(queries, latent, out_grad, segments):
    rows_here = queries.shape[0]
    lat_width = queries.shape[2]
    key_span = WINDOW * rows_here
    lead_rows = key_span - rows_here
    own_block = lax.all_gather(latent, "head", axis=0, tiled=True)
    block_list = [own_block]
    travelling = own_block
    for distance in range(1, WINDOW):
        travelling = shifted(travelling, "ctx", 1)
        block_list.append(travelling)
    key_rows = jnp.concatenate(block_list[::-1], axis=0)
    first_row = lax.axis_index("ctx") * rows_here
    padded_segments = jnp.concatenate([jnp.full((lead_rows,), -1, jnp.int32), segments])
    key_segments = lax.dynamic_slice_in_dim(padded_segments, first_row, key_span, 0)
    query_segments = lax.dynamic_slice_in_dim(segments, first_row, rows_here, 0)
    query_index = first_row + jnp.arange(rows_here, dtype=jnp.int32)
    key_index = first_row - lead_rows + jnp.arange(key_span, dtype=jnp.int32)
    allowed_mask = window_mask(query_index, key_index, query_segments, key_segments)
    query_grad, grad_keys = block_grads(queries, key_rows, out_grad, allowed_mask)
    key_parts = grad_keys.reshape(WINDOW, rows_here, lat_width)
    running = key_parts[WINDOW - 1]
    for distance in range(1, WINDOW):
        running = running + shifted(
            key_parts[WINDOW - 1 - distance].astype(jnp.bfloat16), "ctx", -distance
        ).astype(jnp.float32)
    latent_grad = lax.psum_scatter(
        running.astype(jnp.bfloat16), "head", scatter_dimension=0, tiled=True
    ).astype(jnp.float32)
    return (query_grad, latent_grad)


def solution(mesh):
    in_specs = (P("ctx", "head", None), P(("ctx", "head"), None), P("ctx", "head", None), P())
    out_specs = (P("ctx", "head", None), P(("ctx", "head"), None))
    return jax.shard_map(shards, mesh=mesh, in_specs=in_specs, out_specs=out_specs, check_vma=False)
```

profile of v0, /device:TPU:0, one launch (start us, length us, event | category | flops | bytes accessed | tf_op | source)
XLA Modules:
  0.0 91.7 jit_solution(10103650811644814714)
XLA Ops:
  7.2 0.0 copy-start
  7.2 0.0 reduce-scatter.4.cloned.1.call-start
  7.2 15.5 %all_gather.3 = bf16[128,576]{1,0:T(8,128)(2,1)S(1)} all-gather(bf16[32,576]{1,0:T(8,128)(2,1)} %param.5), channel_id=1, replica_groups=mesh['ctx'=8,'head'=4] {'head'}, dimensions={0}, use_global_device_ids=true | all-gather | bytes 184320 | tf_op jit(solution)/shard_map/all_gather | solution.py:63
  22.7 1.3 %collective-permute-start = (bf16[128,576]{1,0:T(8,128)(2,1)S(1)}, bf16[128,576]{1,0:T(8,128)(2,1)S(1)}, u32[]{:S(2)}, u32[]{:S(2)}) collective-permute-start(bf16[128,576]{1,0:T(8,128)(2,1)S(1)} %all_gather.3), channel_id=1, source_target_pairs={{0,4},{4,8},{8,12},{12,16},{16,20},{20,24},{24,28},{1,5},{5,9},{9,... | collective-permute-start | bytes 442376 | tf_op jit(solution)/shard_map/ppermute | solution.py:15
  24.1 0.8 dynamic_slice.7
  24.8 0.8 pad_dynamic-slice_fusion
  25.6 0.0 collective-permute-done
  25.6 4.8 %collective-permute-start.1 = (bf16[128,576]{1,0:T(8,128)(2,1)S(1)}, bf16[128,576]{1,0:T(8,128)(2,1)S(1)}, u32[]{:S(2)}, u32[]{:S(2)}) collective-permute-start(bf16[128,576]{1,0:T(8,128)(2,1)S(1)} %collective-permute-done), channel_id=1, source_target_pairs={{0,4},{4,8},{8,12},{12,16},{16,20},{20,24},{24,28},{1,5},{5,9},{9,... | collective-permute-start | bytes 442376 | tf_op jit(solution)/shard_map/ppermute | solution.py:15
  30.4 0.1 compare_and_fusion
  30.6 0.9 collective-permute-done.1
  31.4 5.6 %collective-permute-start.2 = (bf16[128,576]{1,0:T(8,128)(2,1)S(1)}, bf16[128,576]{1,0:T(8,128)(2,1)S(1)}, u32[]{:S(2)}, u32[]{:S(2)}) collective-permute-start(bf16[128,576]{1,0:T(8,128)(2,1)S(1)} %collective-permute-done.1), channel_id=1, source_target_pairs={{0,4},{4,8},{8,12},{12,16},{16,20},{20,24},{24,28},{1,5},{5,9},{9,... | collective-permute-start | bytes 442376 | tf_op jit(solution)/shard_map/ppermute | solution.py:15
  37.0 0.2 broadcast_bitcast_fusion
  37.3 0.6 copy.16
  37.9 2.2 %copy.14 = bf16[128,8,576]{2,1,0:T(8,128)(2,1)S(1)} copy(bf16[128,8,576]{0,2,1:T(8,128)(2,1)} %param.4) | data formatting | bytes 2359296 | tf_op args[0]
  40.1 0.0 collective-permute-done.2
  40.3 0.0 copy-start.3
  40.3 1.1 %fusion.3 = (f32[1024]{0:T(1024)S(1)}, f32[512,1024]{1,0:T(8,128)S(1)}) fusion(pred[1024,512]{0,1:T(32,128)(4,1)S(1)} %copy.16, bf16[512,576]{1,0:T(8,128)(2,1)S(1)} %constant_dynamic-update-slice_fusion, bf16[128,8,576]{2,1,0:T(8,128)(2,1)S(1)} %copy.14), kind=kOutput, calls=%fused_computation.8 | convolution fusion | flops 605551616 | bytes 4395008 | tf_op jit(solution)/shard_map/dot_general | solution.py:30
  41.4 0.6 fusion.9
  42.0 0.0 copy-done.3
  42.0 0.0 copy-done
  42.0 1.1 %fusion = (f32[1024]{0:T(1024)S(1)}, f32[512,1024]{1,0:T(8,128)S(1)}) fusion(f32[1024]{0:T(1024)S(1)} %fusion.9, pred[1024,512]{0,1:T(32,128)(4,1)S(1)} %copy.16, f32[1024]{0:T(1024)S(1)} %get-tuple-element.11, f32[512,1024]{1,0:T(8,128)S(1)} %get-tuple-element.12, bf16[128,8,512]{2,1,0:T(8,128)(2,1)S(1)} %copy-done, ...), kind=kOutput, calls=%fused_computation.3 | convolution fusion | flops 540539904 | bytes 6303744 | tf_op jit(solution)/shard_map/dot_general | solution.py:39
  43.1 1.1 %fusion.10 = f32[512,512]{0,1:T(8,128)S(1)} fusion(bf16[128,8,512]{2,1,0:T(8,128)(2,1)S(1)} %copy-done, pred[1024,512]{0,1:T(32,128)(4,1)S(1)} %copy.16, f32[512,1024]{1,0:T(8,128)S(1)} %get-tuple-element.12, f32[1024]{0:T(1024)S(1)} %fusion.9, f32[1024]{0:T(1024)S(1)} %get-tuple-element.11), kind=kOutput, calls=%fused_computation.16 | convolution fusion | flops 540016640 | bytes 4726784 | tf_op jit(solution)/shard_map/dot_general | solution.py:50
  44.2 0.8 fusion.2
  45.0 0.0 copy-start.1
  45.0 0.8 fusion.21
  45.8 0.1 copy-done.1
  46.0 0.0 copy-start.2
  46.0 0.1 fusion.20
  46.0 1.4 %collective-permute-start.5 = (bf16[128,576]{0,1:T(8,128)(2,1)S(1)}, bf16[128,576]{0,1:T(8,128)(2,1)S(1)}, u32[]{:S(2)}, u32[]{:S(2)}) collective-permute-start(bf16[128,576]{0,1:T(8,128)(2,1)S(1)} %get-tuple-element.9), channel_id=1, source_target_pairs={{12,0},{16,4},{20,8},{24,12},{28,16},{13,1},{17,5},{21,9},{25,13},... | collective-permute-start | bytes 442376 | tf_op jit(solution)/shard_map/ppermute | solution.py:15
  47.5 1.3 %collective-permute-start.4 = (bf16[128,576]{0,1:T(8,128)(2,1)S(1)}, bf16[128,576]{0,1:T(8,128)(2,1)S(1)}, u32[]{:S(2)}, u32[]{:S(2)}) collective-permute-start(bf16[128,576]{0,1:T(8,128)(2,1)S(1)} %get-tuple-element.10), channel_id=1, source_target_pairs={{8,0},{12,4},{16,8},{20,12},{24,16},{28,20},{9,1},{13,5},{17,9},{2... | collective-permute-start | bytes 442376 | tf_op jit(solution)/shard_map/ppermute | solution.py:15
  48.8 1.3 %collective-permute-start.3 = (bf16[128,576]{0,1:T(8,128)(2,1)S(1)}, bf16[128,576]{0,1:T(8,128)(2,1)S(1)}, u32[]{:S(2)}, u32[]{:S(2)}) collective-permute-start(bf16[128,576]{0,1:T(8,128)(2,1)S(1)} %get-tuple-element.8), channel_id=1, source_target_pairs={{4,0},{8,4},{12,8},{16,12},{20,16},{24,20},{28,24},{5,1},{9,5},{13... | collective-permute-start | bytes 442376 | tf_op jit(solution)/shard_map/ppermute | solution.py:15
  50.1 7.6 %collective-permute-done.5 = bf16[128,576]{0,1:T(8,128)(2,1)S(1)} collective-permute-done((bf16[128,576]{0,1:T(8,128)(2,1)S(1)}, bf16[128,576]{0,1:T(8,128)(2,1)S(1)}, u32[]{:S(2)}, u32[]{:S(2)}) %collective-permute-start.5) | collective-permute-done | bytes 147488 | tf_op jit(solution)/shard_map/ppermute | solution.py:15
  57.6 0.4 collective-permute-done.4
  58.0 0.0 collective-permute-done.3
  58.1 0.1 fusion.18
  58.1 0.8 copy.20
  59.0 0.0 reduce-scatter.4.cloned.1.call-update
  59.0 0.0 copy-done.2
  59.0 1.9 %multiply_convert_fusion = bf16[1024,576]{0,1:T(8,128)(2,1)S(1)} fusion(bf16[1024,512]{0,1:T(8,128)(2,1)S(1)} %copy-done.2, bf16[512,576]{1,0:T(8,128)(2,1)} %copy-done.3), kind=kOutput, calls=%fused_computation | convolution fusion | flops 605159424 | bytes 2818048 | tf_op jit(solution)/shard_map/dot_general | solution.py:45
  60.9 0.7 copy.17
  61.6 1.8 %copy.18 = bf16[128,8,576]{0,2,1:T(8,128)(2,1)} copy(bf16[128,8,576]{2,1,0:T(8,128)(2,1)S(1)} %bitcast.50) | data formatting | bytes 2359296
  63.4 19.8 %reduce-scatter.4.cloned.1.call-done = bf16[32,576]{1,0:T(8,128)(2,1)} async-done(((bf16[128,576]{1,0:T(8,128)(2,1)}), bf16[32,576]{1,0:T(8,128)(2,1)}) %reduce-scatter.4.cloned.1.call-update) | async-done | bytes 36880
  83.2 0.9 copy.21
  84.1 0.8 copy.19
  (6 shorter events, 0.1 us)
Async XLA Ops:
  7.2 34.8 %copy-start = (bf16[128,8,512]{2,1,0:T(8,128)(2,1)S(1)}, bf16[128,8,512]{2,1,0:T(8,128)(2,1)}, u32[]{:S(2)}) copy-start(bf16[128,8,512]{2,1,0:T(8,128)(2,1)} %param.6) | copy-start | bytes 3145732
  7.2 76.0 %reduce-scatter.4.cloned.1.call-start = ((), (), s32[]{:S(2)}) async-start(), calls=%async_computation.1 | async-start | bytes 204800
  22.7 2.9 %collective-permute-start = (bf16[128,576]{1,0:T(8,128)(2,1)S(1)}, bf16[128,576]{1,0:T(8,128)(2,1)S(1)}, u32[]{:S(2)}, u32[]{:S(2)}) collective-permute-start(bf16[128,576]{1,0:T(8,128)(2,1)S(1)} %all_gather.3), channel_id=1, source_target_pairs={{0,4},{4,8},{8,12},{12,16},{16,20},{20,24},{24,28},{1,5},{5,9},{9,... | collective-permute-start | bytes 442376 | tf_op jit(solution)/shard_map/ppermute | solution.py:15
  25.6 5.8 %collective-permute-start.1 = (bf16[128,576]{1,0:T(8,128)(2,1)S(1)}, bf16[128,576]{1,0:T(8,128)(2,1)S(1)}, u32[]{:S(2)}, u32[]{:S(2)}) collective-permute-start(bf16[128,576]{1,0:T(8,128)(2,1)S(1)} %collective-permute-done), channel_id=1, source_target_pairs={{0,4},{4,8},{8,12},{12,16},{16,20},{20,24},{24,28},{1,5},{5,9},{9,... | collective-permute-start | bytes 442376 | tf_op jit(solution)/shard_map/ppermute | solution.py:15
  31.4 8.7 %collective-permute-start.2 = (bf16[128,576]{1,0:T(8,128)(2,1)S(1)}, bf16[128,576]{1,0:T(8,128)(2,1)S(1)}, u32[]{:S(2)}, u32[]{:S(2)}) collective-permute-start(bf16[128,576]{1,0:T(8,128)(2,1)S(1)} %collective-permute-done.1), channel_id=1, source_target_pairs={{0,4},{4,8},{8,12},{12,16},{16,20},{20,24},{24,28},{1,5},{5,9},{9,... | collective-permute-start | bytes 442376 | tf_op jit(solution)/shard_map/ppermute | solution.py:15
  40.3 1.7 %copy-start.3 = (bf16[512,576]{1,0:T(8,128)(2,1)}, bf16[512,576]{1,0:T(8,128)(2,1)S(1)}, u32[]{:S(2)}) copy-start(bf16[512,576]{1,0:T(8,128)(2,1)S(1)} %constant_dynamic-update-slice_fusion) | copy-start | bytes 1769476
  45.0 1.0 %copy-start.1 = (bf16[1024,512]{0,1:T(8,128)(2,1)}, bf16[1024,512]{0,1:T(8,128)(2,1)S(1)}, u32[]{:S(2)}) copy-start(bf16[1024,512]{0,1:T(8,128)(2,1)S(1)} %fusion.2) | copy-start | bytes 3145732
  46.0 13.0 %copy-start.2 = (bf16[1024,512]{0,1:T(8,128)(2,1)S(1)}, bf16[1024,512]{0,1:T(8,128)(2,1)}, u32[]{:S(2)}) copy-start(bf16[1024,512]{0,1:T(8,128)(2,1)} %copy-done.1) | copy-start | bytes 3145732
  46.0 11.6 %collective-permute-start.5 = (bf16[128,576]{0,1:T(8,128)(2,1)S(1)}, bf16[128,576]{0,1:T(8,128)(2,1)S(1)}, u32[]{:S(2)}, u32[]{:S(2)}) collective-permute-start(bf16[128,576]{0,1:T(8,128)(2,1)S(1)} %get-tuple-element.9), channel_id=1, source_target_pairs={{12,0},{16,4},{20,8},{24,12},{28,16},{13,1},{17,5},{21,9},{25,13},... | collective-permute-start | bytes 442376 | tf_op jit(solution)/shard_map/ppermute | solution.py:15
  47.5 10.6 %collective-permute-start.4 = (bf16[128,576]{0,1:T(8,128)(2,1)S(1)}, bf16[128,576]{0,1:T(8,128)(2,1)S(1)}, u32[]{:S(2)}, u32[]{:S(2)}) collective-permute-start(bf16[128,576]{0,1:T(8,128)(2,1)S(1)} %get-tuple-element.10), channel_id=1, source_target_pairs={{8,0},{12,4},{16,8},{20,12},{24,16},{28,20},{9,1},{13,5},{17,9},{2... | collective-permute-start | bytes 442376 | tf_op jit(solution)/shard_map/ppermute | solution.py:15
  48.8 9.3 %collective-permute-start.3 = (bf16[128,576]{0,1:T(8,128)(2,1)S(1)}, bf16[128,576]{0,1:T(8,128)(2,1)S(1)}, u32[]{:S(2)}, u32[]{:S(2)}) collective-permute-start(bf16[128,576]{0,1:T(8,128)(2,1)S(1)} %get-tuple-element.8), channel_id=1, source_target_pairs={{4,0},{8,4},{12,8},{16,12},{20,16},{24,20},{28,24},{5,1},{9,5},{13... | collective-permute-start | bytes 442376 | tf_op jit(solution)/shard_map/ppermute | solution.py:15
Sparse Core Ops, SparseCore 0:
  59.1 24.0 reduce-scatter.3
where the time goes:
time: 92.2 us; the launch traced here: 91.7 us
  waiting for transfers between devices  28.6 us (31%)
  starting transfers between devices  15.7 us (17%)
  blocking collectives  15.5 us (17%)
  between operations  14.3 us (16%)
  local copies, waits for them, and re-layouts  9.13 us (10%)
  matrix products  5.99 us (6%)
  other arithmetic  2.42 us (3%)
    unnamed x2, waiting for transfers between devices  19.8 us
    ppermute x6, starting transfers between devices, shifted(): return lax.ppermute(value, axis, pairs)  15.7 us
    all_gather x1, blocking collectives, shards(): own_block = lax.all_gather(latent, 'head', axis=0, tiled=True)  15.5 us
    ppermute x6, waiting for transfers between devices, shifted(): return lax.ppermute(value, axis, pairs)  8.84 us
    unnamed x16, local copies, waits for them, and re-layouts  6.69 us
    dot_general x1, matrix products, block_grads(): jnp.dot(grad_scores, key_rows, preferred_element_type=jnp.float32)  1.91 us
  transfers between devices with their start and end apart: 7, of which 4 were waited for; matrix products, arithmetic and copies ran while one was open for 10% of the time, Pallas kernels for 0%

commit v1 on v0

v1 whole, which is shorter than its diff:
```python
import functools

import jax
import jax.numpy as jnp
from jax import lax
from jax.experimental import pallas as pl
from jax.experimental.pallas import tpu as pltpu
from jax.sharding import PartitionSpec as P

WINDOW = 4
BACK3, BACK1, BACK2, OWN = 0, 1, 2, 3
DISTANCE = (3, 1, 2, 0)

score_scale = 192.0 ** (-0.5)


def when(cond):
    if cond is None:
        return lambda f: f()
    return pl.when(cond)


def flat(value, rows):
    if value.dtype == jnp.bfloat16 and value.shape[-2] % 16:
        return value.astype(jnp.float32).reshape(rows, value.shape[-1]).astype(jnp.bfloat16)
    return value.reshape(rows, value.shape[-1])


def kernel(
    n, heads, q_hbm, lat_ref, g_hbm, seg_ref, dq_hbm, dlat_ref,
    q3, g3, gw, qf, gf, kv, kf, kseg, allow, pt, dst, dk, sb, rp, r2, r3, zb, dq3,
    io_sem, g_send, g_recv, r_send, r_recv,
):
    c = lax.axis_index("ctx")
    h = lax.axis_index("head")
    odd = c % 2 == 1
    even = c % 2 == 0
    partner = (c + 1 - 2 * (c % 2), h)
    per, width, rows = q_hbm.shape
    rank = gf.shape[1]
    flat_rows = rows * per
    keys = WINDOW * rows
    f32, bf16 = jnp.float32, jnp.bfloat16

    def remote(src, dst_ref, ssem, rsem, peer):
        return pltpu.make_async_remote_copy(
            src_ref=src, dst_ref=dst_ref, send_sem=ssem, recv_sem=rsem,
            device_id=peer, device_id_type=pl.DeviceIdType.MESH,
        )

    def arrived(ref, sem):
        remote(ref, ref, sem, sem, partner).wait_recv()

    def sent(ref, sem):
        remote(ref, ref, sem, sem, partner).wait_send()

    load_q = pltpu.make_async_copy(q_hbm, q3, io_sem.at[0])
    load_g = pltpu.make_async_copy(g_hbm, g3, io_sem.at[1])
    load_g.start()
    load_q.start()

    up2, down2 = c + 2 < n, c >= 2
    up3, down3 = odd & (c + 3 < n), even & (c >= 3)
    peers = [(None, (c, (h + k) % heads)) for k in range(1, heads)]
    peers += [(None, partner), (up2, (c + 2, h)), (down2, (c - 2, h)),
              (up3, (c + 3, h)), (down3, (c - 3, h))]
    barrier = pltpu.get_barrier_semaphore()
    for cond, peer in peers:
        @when(cond)
        def _():
            pl.semaphore_signal(
                barrier, inc=1, device_id=peer, device_id_type=pl.DeviceIdType.MESH
            )
    flags = [cond for cond, _ in peers if cond is not None]
    pl.semaphore_wait(barrier, len(peers) - len(flags) + sum(f.astype(jnp.int32) for f in flags))

    def onward(src, s):
        @pl.when(up2)
        def _():
            remote(src, kv.at[BACK2, s], g_send.at[1, s], g_recv.at[BACK2, s], (c + 2, h)).start()

        @pl.when(up3)
        def _():
            remote(src, kv.at[BACK3, s], g_send.at[2, s], g_recv.at[BACK3, s], (c + 3, h)).start()

        @pl.when(even)
        def _():
            remote(src, kv.at[BACK1, s], g_send.at[2, s], g_recv.at[BACK1, s], partner).start()

    def relay(s):
        @pl.when(down2)
        def _():
            arrived(kv.at[BACK2, s], g_recv.at[BACK2, s])

            @pl.when(even)
            def _():
                remote(kv.at[BACK2, s], kv.at[BACK3, s], g_send.at[3, s], g_recv.at[BACK3, s], partner).start()

            @pl.when(odd)
            def _():
                remote(kv.at[BACK2, s], kv.at[BACK1, s], g_send.at[3, s], g_recv.at[BACK1, s], partner).start()

    for k in range(1, heads):
        remote(lat_ref, kv.at[OWN, h], g_send.at[0, k], g_recv.at[OWN, h], (c, (h + k) % heads)).start()
    onward(lat_ref, h)
    kv[OWN, h] = lat_ref[...]

    for place, cond in ((BACK1, c < 1), (BACK2, c < 2), (BACK3, c < 3)):
        @pl.when(cond)
        def _():
            kv[place] = jnp.zeros(kv.shape[1:], kv.dtype)

    load_g.wait()
    lanes = gw.shape[2]
    for i in range(rank // lanes):
        part = pl.ds(i * lanes, lanes)
        gw[i] = g3[:, :, part].astype(f32).reshape(flat_rows, lanes)
        for j in range(per):
            gf[pl.ds(j * rows, rows), part] = gw[i, pl.ds(j, rows, stride=per), :].astype(bf16)

    for k in range(1, heads):
        s = (h + heads - k) % heads
        arrived(kv.at[OWN, s], g_recv.at[OWN, s])
        onward(kv.at[OWN, s], s)
        relay((s + 1) % heads)
    relay((h + 1) % heads)

    load_q.wait()
    for j in range(per):
        qf[:, pl.ds(j * rows, rows)] = q3[j]

    for place, distance in enumerate(DISTANCE):
        row = seg_ref[pl.ds(jnp.maximum(c - distance, 0), 1), :].astype(f32)
        row = jnp.where(c >= distance, row, -1.0)
        kseg[pl.ds(place * rows, rows), :] = jnp.broadcast_to(row, (rows, rows)).T
    qseg = seg_ref[pl.ds(c, 1), :].astype(f32)
    key_at = lax.broadcasted_iota(jnp.int32, (keys, rows), 0) - OWN * rows
    token_at = lax.broadcasted_iota(jnp.int32, (keys, rows), 1)
    allow[...] = ((kseg[...] == qseg) & (key_at <= token_at)).astype(f32)

    for s in range(heads):
        @pl.when(c >= 1)
        def _():
            arrived(kv.at[BACK1, s], g_recv.at[BACK1, s])

        @pl.when(c >= 3)
        def _():
            arrived(kv.at[BACK3, s], g_recv.at[BACK3, s])
    kf[...] = flat(kv[...], keys)

    nt = (((1,), (1,)), ((), ()))
    tn = (((0,), (0,)), ((), ()))
    cols = rows * 2
    for start in range(0, flat_rows, cols):
        part = pl.ds(start, cols)
        st = score_scale * jnp.dot(kf[...], qf[:, part], preferred_element_type=f32)
        gt = lax.dot_general(kf[:, :rank], gf[part, :], nt, preferred_element_type=f32)
        allowed = jnp.concatenate([allow[...]] * (cols // rows), axis=1) > 0.0
        st = jnp.where(allowed, st, -1e30)
        top = jnp.max(st, axis=0, keepdims=True)
        w = jnp.where(allowed, jnp.exp(st - top), 0.0)
        probs = w * (1.0 / jnp.sum(w, axis=0, keepdims=True))
        pt[:, part] = probs.astype(bf16)
        delta = jnp.sum(probs * gt, axis=0, keepdims=True)
        dst[:, part] = (probs * (gt - delta)).astype(bf16)

    def key_grads(first):
        part = pl.ds(first * rows, 2 * rows)
        from_scores = lax.dot_general(dst[part, :], qf[...], nt, preferred_element_type=f32)
        from_values = jnp.dot(pt[part, :], gf[...], preferred_element_type=f32)
        total = jnp.concatenate(
            [score_scale * from_scores[:, :rank] + from_values, score_scale * from_scores[:, rank:]],
            axis=1,
        )
        dk[pl.ds(first, 2)] = total.reshape((2,) + dk.shape[1:])

    order = [(h + k) % heads for k in range(1, heads + 1)]
    key_grads(BACK3)
    sb[pl.ds(BACK3, 2)] = dk[pl.ds(BACK3, 2)].astype(bf16)
    for s in order:
        @pl.when(even & down2)
        def _():
            remote(sb.at[BACK1, s], rp.at[0, s], r_send.at[0, s], r_recv.at[0, s], partner).start()

        @pl.when(odd & (c >= 3))
        def _():
            remote(sb.at[BACK3, s], rp.at[0, s], r_send.at[0, s], r_recv.at[0, s], partner).start()

        @pl.when(odd)
        def _():
            remote(sb.at[BACK1, s], rp.at[1, s], r_send.at[1, s], r_recv.at[1, s], partner).start()

        @pl.when(down3)
        def _():
            remote(sb.at[BACK3, s], r3.at[s], r_send.at[1, s], r_recv.at[3, s], (c - 3, h)).start()
    key_grads(BACK2)
    for s in order:
        @pl.when(down2)
        def _():
            arrived(rp.at[0, s], r_recv.at[0, s])
            sb[BACK2, s] = (dk[BACK2, s] + rp[0, s].astype(f32)).astype(bf16)
            remote(sb.at[BACK2, s], r2.at[s], r_send.at[2, s], r_recv.at[2, s], (c - 2, h)).start()

    for start in range(0, flat_rows, cols):
        dq = score_scale * lax.dot_general(kf[...], dst[:, pl.ds(start, cols)], tn, preferred_element_type=f32)
        for j in range(cols // rows):
            dq3[start // rows + j] = dq[:, j * rows:(j + 1) * rows].astype(bf16)
    store_q = pltpu.make_async_copy(dq3, dq_hbm, io_sem.at[0])
    store_q.start()

    for k, s in enumerate(order):
        @pl.when(even)
        def _():
            arrived(rp.at[1, s], r_recv.at[1, s])
            dk[OWN, s] += rp[1, s].astype(f32)

        @pl.when(up2)
        def _():
            arrived(r2.at[s], r_recv.at[2, s])
            dk[OWN, s] += r2[s].astype(f32)

        @pl.when(up3)
        def _():
            arrived(r3.at[s], r_recv.at[3, s])
            dk[OWN, s] += r3[s].astype(f32)

        if k < heads - 1:
            sb[OWN, s] = dk[OWN, s].astype(bf16)
            remote(sb.at[OWN, s], zb.at[h], r_send.at[3, s], r_recv.at[4, h], (c, s)).start()
    total = dk[OWN, h]
    for s in order[-2::-1]:
        arrived(zb.at[s], r_recv.at[4, s])
        total = total + zb[s].astype(f32)
    dlat_ref[...] = total

    shard = zb.at[0]
    for k in range(1, heads):
        sent(lat_ref, g_send.at[0, k])
        sent(shard, r_send.at[3, order[k - 1]])
    for s in range(heads):
        for cond, sem in (
            (up2, g_send.at[1, s]), (up3, g_send.at[2, s]), (even, g_send.at[2, s]),
            (down2, g_send.at[3, s]), (even & down2, r_send.at[0, s]), (odd & (c >= 3), r_send.at[0, s]),
            (odd, r_send.at[1, s]), (down3, r_send.at[1, s]), (down2, r_send.at[2, s]),
        ):
            @pl.when(cond)
            def _():
                sent(shard, sem)
    store_q.wait()


def shards(n, heads, queries, latent, out_grad, segments):
    rows, per, width = queries.shape
    rank = out_grad.shape[2]
    height = latent.shape[0]
    f32, bf16 = jnp.float32, jnp.bfloat16
    flat_rows, keys = rows * per, WINDOW * rows
    vmem = pl.BlockSpec(memory_space=pltpu.VMEM)
    hbm = pl.BlockSpec(memory_space=pl.ANY)
    query_grad, latent_grad = pl.pallas_call(
        functools.partial(kernel, n, heads),
        out_shape=(
            jax.ShapeDtypeStruct((per, width, rows), bf16),
            jax.ShapeDtypeStruct(latent.shape, f32),
        ),
        in_specs=[hbm, vmem, hbm, vmem],
        out_specs=(hbm, vmem),
        scratch_shapes=[
            pltpu.VMEM((per, width, rows), bf16),
            pltpu.VMEM((rows, per, rank), bf16),
            pltpu.VMEM((rank // 128, flat_rows, 128), f32),
            pltpu.VMEM((width, flat_rows), bf16),
            pltpu.VMEM((flat_rows, rank), bf16),
            pltpu.VMEM((WINDOW, heads, height, width), bf16),
            pltpu.VMEM((keys, width), bf16),
            pltpu.VMEM((keys, rows), f32),
            pltpu.VMEM((keys, rows), f32),
            pltpu.VMEM((keys, flat_rows), bf16),
            pltpu.VMEM((keys, flat_rows), bf16),
            pltpu.VMEM((WINDOW, heads, height, width), f32),
            pltpu.VMEM((WINDOW, heads, height, width), bf16),
            pltpu.VMEM((2, heads, height, width), bf16),
            pltpu.VMEM((heads, height, width), bf16),
            pltpu.VMEM((heads, height, width), bf16),
            pltpu.VMEM((heads, height, width), bf16),
            pltpu.VMEM((per, width, rows), bf16),
            pltpu.SemaphoreType.DMA((2,)),
            pltpu.SemaphoreType.DMA((4, heads)),
            pltpu.SemaphoreType.DMA((4, heads)),
            pltpu.SemaphoreType.DMA((4, heads)),
            pltpu.SemaphoreType.DMA((5, heads)),
        ],
        compiler_params=pltpu.CompilerParams(
            collective_id=0, has_side_effects=True, vmem_limit_bytes=67043328
        ),
    )(queries.transpose(1, 2, 0), latent, out_grad, segments.reshape(-1, rows))
    return query_grad.transpose(2, 0, 1), latent_grad


def solution(mesh):
    n, heads = mesh.shape["ctx"], mesh.shape["head"]
    in_specs = (P("ctx", "head", None), P(("ctx", "head"), None), P("ctx", "head", None), P())
    out_specs = (P("ctx", "head", None), P(("ctx", "head"), None))
    return jax.shard_map(
        functools.partial(shards, n, heads),
        mesh=mesh, in_specs=in_specs, out_specs=out_specs, check_vma=False,
    )
```

time: 92.2 us -> 34.1 us (0.37)
  the two profiles are of different devices: /device:TPU:0 before, /device:TPU:3 now
where the time goes in v1:
time: 34.1 us; the launch traced here: 33.9 us
  Pallas kernels  30.2 us (89%)
  local copies, waits for them, and re-layouts  3.04 us (9%)
  between operations  0.65 us (2%)
    pallas_call x1, Pallas kernels, shards(): pl.pallas_call(functools.partial(kernel, n, heads), out_shape=(jax.ShapeD...  30.2 us
    unnamed x4, local copies, waits for them, and re-layouts  3.04 us

profile of v1, /device:TPU:3, one launch (start us, length us, event | category | flops | bytes accessed | tf_op | source)
XLA Modules:
  0.0 33.9 jit_solution(9608911352033120768)
XLA Ops:
  0.6 30.2 %shard_map.59 = (bf16[8,576,128]{2,1,0:T(8,128)(2,1)}, f32[32,576]{1,0:T(8,128)}) custom-call(bf16[8,576,128]{2,1,0:T(8,128)(2,1)} %bitcast.3, bf16[32,576]{1,0:T(8,128)(2,1)} %lat_ref.1, bf16[128,8,512]{2,1,0:T(8,128)(2,1)} %g_hbm.1, s32[8,128]{1,0:T(8,128)} %bitcast.5), custom_call_target="tpu_custom_call" | custom-call | tf_op jit(solution)/shard_map/pallas_call | solution.py:260
  30.8 0.0 copy-start
  30.8 2.4 %copy.8 = bf16[128,8,576]{0,2,1:T(8,128)(2,1)} copy(bf16[128,8,576]{0,2,1:T(8,128)(2,1)} %bitcast.4) | data formatting | bytes 2359296
  33.2 0.0 copy-done
  33.3 0.6 %copy.9 = f32[32,576]{1,0:T(8,128)} copy(f32[32,576]{1,0:T(8,128)S(1)} %copy-done) | data formatting | bytes 147456
Async XLA Ops:
  30.8 2.4 %copy-start = (f32[32,576]{1,0:T(8,128)S(1)}, f32[32,576]{1,0:T(8,128)}, u32[]{:S(2)}) copy-start(f32[32,576]{1,0:T(8,128)} %get-tuple-element.9) | copy-start | bytes 221188

commit v2 on v1

--- a/solution.py
+++ b/solution.py
@@ -27,8 +27,8 @@
 
 
 def kernel(
-    n, heads, q_hbm, lat_ref, g_hbm, seg_ref, dq_hbm, dlat_ref,
-    q3, g3, gw, qf, gf, kv, kf, kseg, allow, pt, dst, dk, sb, rp, r2, r3, zb, dq3,
+    n, heads, q_hbm, lat_ref, g_hbm, seg_ref, dq3, dlat_ref,
+    q3, g3, gw, qf, gf, kv, kf, kseg, allow, pt, dst, dk, sb, rp, r2, r3, zb,
     io_sem, g_send, g_recv, r_send, r_recv,
 ):
     c = lax.axis_index("ctx")
@@ -205,8 +205,6 @@
         dq = score_scale * lax.dot_general(kf[...], dst[:, pl.ds(start, cols)], tn, preferred_element_type=f32)
         for j in range(cols // rows):
             dq3[start // rows + j] = dq[:, j * rows:(j + 1) * rows].astype(bf16)
-    store_q = pltpu.make_async_copy(dq3, dq_hbm, io_sem.at[0])
-    store_q.start()
 
     for k, s in enumerate(order):
         @pl.when(even)
@@ -246,7 +244,22 @@
             @pl.when(cond)
             def _():
                 sent(shard, sem)
-    store_q.wait()
+
+
+def store_kernel(dq_in, dlat_in, dq_hbm, dlat_hbm, dq_ref, dlat_ref, sems):
+    count = dq_ref.shape[0]
+    pieces = [(dlat_in, dlat_ref, dlat_hbm)]
+    for j in range(count):
+        pieces.append((dq_in.at[j], dq_ref.at[j], dq_hbm.at[j]))
+    loads = [pltpu.make_async_copy(p[0], p[1], sems.at[0, i]) for i, p in enumerate(pieces)]
+    stores = [pltpu.make_async_copy(p[1], p[2], sems.at[1, i]) for i, p in enumerate(pieces)]
+    for load in loads:
+        load.start()
+    for load, store in zip(loads, stores):
+        load.wait()
+        store.start()
+    for store in stores:
+        store.wait()
 
 
 def shards(n, heads, queries, latent, out_grad, segments):
@@ -256,7 +269,7 @@
     f32, bf16 = jnp.float32, jnp.bfloat16
     flat_rows, keys = rows * per, WINDOW * rows
     vmem = pl.BlockSpec(memory_space=pltpu.VMEM)
-    hbm = pl.BlockSpec(memory_space=pl.ANY)
+    hbm = pl.BlockSpec(memory_space=pltpu.HBM)
     query_grad, latent_grad = pl.pallas_call(
         functools.partial(kernel, n, heads),
         out_shape=(
@@ -264,7 +277,7 @@
             jax.ShapeDtypeStruct(latent.shape, f32),
         ),
         in_specs=[hbm, vmem, hbm, vmem],
-        out_specs=(hbm, vmem),
+        out_specs=(vmem, vmem),
         scratch_shapes=[
             pltpu.VMEM((per, width, rows), bf16),
             pltpu.VMEM((rows, per, rank), bf16),
@@ -283,7 +296,6 @@
             pltpu.VMEM((heads, height, width), bf16),
             pltpu.VMEM((heads, height, width), bf16),
             pltpu.VMEM((heads, height, width), bf16),
-            pltpu.VMEM((per, width, rows), bf16),
             pltpu.SemaphoreType.DMA((2,)),
             pltpu.SemaphoreType.DMA((4, heads)),
             pltpu.SemaphoreType.DMA((4, heads)),
@@ -294,6 +306,21 @@
             collective_id=0, has_side_effects=True, vmem_limit_bytes=67043328
         ),
     )(queries.transpose(1, 2, 0), latent, out_grad, segments.reshape(-1, rows))
+    query_grad, latent_grad = pl.pallas_call(
+        store_kernel,
+        out_shape=(
+            jax.ShapeDtypeStruct(query_grad.shape, bf16),
+            jax.ShapeDtypeStruct(latent.shape, f32),
+        ),
+        in_specs=[hbm, hbm],
+        out_specs=(hbm, hbm),
+        scratch_shapes=[
+            pltpu.VMEM((per, width, rows), bf16),
+            pltpu.VMEM(latent.shape, f32),
+            pltpu.SemaphoreType.DMA((2, per + 1)),
+        ],
+        compiler_params=pltpu.CompilerParams(vmem_limit_bytes=67043328),
+    )(query_grad, latent_grad)
     return query_grad.transpose(2, 0, 1), latent_grad
 
 

time: 34.1 us -> 33.6 us (0.985)
  local copies, waits for them, and re-layouts: 3.04 us -> 0 us
  Pallas kernels: 30.2 us -> 32.8 us
    unnamed x4 -> x0, local copies, waits for them, and re-layouts: 3.04 us -> none
    pallas_call x0 -> x1, Pallas kernels: none -> 2.18 us  [shards(): pl.pallas_call(store_kernel, out_shape=(jax.ShapeDtypeStruct(query_grad.s...]
    pallas_call x1, Pallas kernels: 30.2 us -> 30.6 us  [shards(): pl.pallas_call(functools.partial(kernel, n, heads), out_shape=(jax.ShapeD...]
where the time goes in v2:
time: 33.6 us; the launch traced here: 33.4 us
  Pallas kernels  32.8 us (98%)
  between operations  0.64 us (2%)
    pallas_call x1, Pallas kernels, shards(): pl.pallas_call(functools.partial(kernel, n, heads), out_shape=(jax.ShapeD...  30.6 us
    pallas_call x1, Pallas kernels, shards(): pl.pallas_call(store_kernel, out_shape=(jax.ShapeDtypeStruct(query_grad.s...  2.18 us

profile of v2, /device:TPU:3, one launch (start us, length us, event | category | flops | bytes accessed | tf_op | source)
XLA Modules:
  0.0 33.4 jit_solution(17681947323782283392)
XLA Ops:
  0.6 30.6 %shard_map.59 = (bf16[8,576,128]{2,1,0:T(8,128)(2,1)}, f32[32,576]{1,0:T(8,128)}) custom-call(bf16[8,576,128]{2,1,0:T(8,128)(2,1)} %bitcast.3, bf16[32,576]{1,0:T(8,128)(2,1)} %lat_ref.1, bf16[128,8,512]{2,1,0:T(8,128)(2,1)} %g_hbm.1, s32[8,128]{1,0:T(8,128)} %bitcast.4), custom_call_target="tpu_custom_call" | custom-call | tf_op jit(solution)/shard_map/pallas_call | solution.py:273
  31.3 2.2 %shard_map.60 = (bf16[8,576,128]{2,1,0:T(8,128)(2,1)}, f32[32,576]{1,0:T(8,128)}) custom-call(bf16[8,576,128]{2,1,0:T(8,128)(2,1)} %get-tuple-element.6.dq_in, f32[32,576]{1,0:T(8,128)} %get-tuple-element.7.dlat_in), custom_call_target="tpu_custom_call" | custom-call | tf_op jit(solution)/shard_map/pallas_call | solution.py:309
